TPU v7x, 256 devices: a whole 4x4x8 slice. The times are simulated.
256 devices in a mesh: grp: 64 (over z, y_hi, x), rep: 4 (over y_lo, core).
Axes of the slice: x: 4, y: 4 (y_hi: 2, y_lo: 2; y = y_hi * 2 + y_lo), z: 8, core: 2. Of those that a mesh axis runs over, the one named last changes fastest.
Arguments:
- embeddings: bfloat16 [65536, 1024], P(('grp', 'rep')), may hold values from -15 to 15
- scales: float32 [65536, 8], P(('grp', 'rep')), may hold values from 0.05 to 0.5
- cluster: int32 [65536], P(('grp', 'rep')), may hold values from 0 to 767, as said below
- cluster_rank: int32 [65536], P(('grp', 'rep')), may hold values from 0 to 63, as said below
Outputs:
- best_cosine: float32 [65536], P(('grp', 'rep'))
Inputs may be any that keep to these rules, and one draw needn't show every extreme that they name: cluster // 12 names the owner of a row's cluster among 64 and cluster % 12 its place there; clusters of different shards are different even with equal numbers. Among the rows of one device at most 12 have the same owner, and in every draw some owner is named by exactly 12 rows of every device of its shard. `cluster_rank`: within one cluster the ranks of its rows are 0 to its size minus 1, each once; a cluster holds at most 64 rows, and in every draw some cluster holds exactly 64.
All inputs are finite; a program needn't handle non-finite values.
Results may differ from a plain program's by a relative error of at most 0.00035.
The roundings to bfloat16 on the way count: a program that leaves them out, or rounds other values in their place, can miss the bound.
Values may be sent and summed in bfloat16 or wider, within the bound.
A program may use at most 64 MiB of HBM per device.

v0:
```python
import jax
import jax.numpy as jnp
from jax import lax
from jax.sharding import PartitionSpec as P

CMAX = 64
STEPS = 5


COV_EPS = 0.001
UNIT_EPS = 1e-06
EXACT_MODE = lax.Precision.HIGHEST


def dequantize(embeddings, scales):
    row_count, feat_dim = embeddings.shape
    num_blocks = scales.shape[1]
    grouped = (
        embeddings.astype(jnp.float32).reshape(row_count, num_blocks, feat_dim // num_blocks)
        * scales[:, :, None]
    )
    return grouped.reshape(row_count, feat_dim).astype(jnp.bfloat16)


def covariance(gram_sum, column_total, row_total):
    average = column_total / row_total
    feat_dim = gram_sum.shape[0]
    centred = (
        gram_sum / row_total
        - average[:, None] * average[None, :]
        + COV_EPS * jnp.eye(feat_dim, dtype=jnp.float32)
    )
    normed = centred / jnp.sqrt(jnp.sum(centred * centred))
    return (average, normed)


def newton_rows(normed_rows, current_rows, first_full, spread):
    whole = first_full
    for repeat in range(STEPS - 1):
        if repeat > 0 or first_full is None:
            whole = spread(current_rows)
        product = jnp.dot(normed_rows, whole, precision=EXACT_MODE)
        product = jnp.dot(product, whole, precision=EXACT_MODE)
        product = jnp.dot(product, whole, precision=EXACT_MODE)
        current_rows = 1.5 * current_rows - 0.5 * product
    return current_rows


def whiten(values, inverse_root, average):
    offset = jnp.dot(average[None, :], inverse_root.astype(jnp.float32), precision=EXACT_MODE)
    projected = jnp.dot(values, inverse_root, preferred_element_type=jnp.float32) - offset
    energy = jnp.sum(projected * projected, axis=1, keepdims=True)
    return (projected * lax.rsqrt(energy + UNIT_EPS)).astype(jnp.bfloat16)


def best_within(table, occupied, cluster_count):
    feat_dim = table.shape[1]
    tile_rows = table.reshape(cluster_count, CMAX, feat_dim)
    similar = jnp.einsum("cmd,cnd->cmn", tile_rows, tile_rows, preferred_element_type=jnp.float32)
    present = occupied.reshape(cluster_count, CMAX)
    distinct = lax.broadcasted_iota(jnp.int32, (1, CMAX, CMAX), 1) != lax.broadcasted_iota(
        jnp.int32, (1, CMAX, CMAX), 2
    )
    allowed = present[:, :, None] & present[:, None, :] & distinct
    highest = jnp.max(jnp.where(allowed, similar, -jnp.inf), axis=2)
    return jnp.maximum(highest, -1.0).reshape(cluster_count * CMAX)


def local(embeddings, scales, cluster, cluster_rank):
    row_count, feat_dim = embeddings.shape
    values = dequantize(embeddings, scales)
    row_total = row_count * lax.axis_size("grp") * lax.axis_size("rep")
    column_part = jnp.sum(values, axis=0, dtype=jnp.float32)
    gram_sum, column_total = lax.psum(
        (
            lax.dot_general(
                values, values, (((0,), (0,)), ((), ())), preferred_element_type=jnp.float32
            ),
            column_part,
        ),
        ("grp", "rep"),
    )
    average, normed = covariance(gram_sum, column_total, row_total)
    share_rows = feat_dim // lax.axis_size("rep")
    first_row = lax.axis_index("rep") * share_rows
    first_full = 1.5 * jnp.eye(feat_dim, dtype=jnp.float32) - 0.5 * normed
    final_rows = newton_rows(
        lax.dynamic_slice_in_dim(normed, first_row, share_rows, 0),
        lax.dynamic_slice_in_dim(first_full, first_row, share_rows, 0),
        first_full,
        lambda slab_rows: lax.all_gather(slab_rows, "rep", axis=0, tiled=True),
    )
    inverse_root = lax.all_gather(final_rows.astype(jnp.bfloat16), "rep", axis=0, tiled=True)
    owner_count = lax.axis_size("grp")
    slot_rows = 3 * row_count // owner_count
    cluster_count = 3 * row_count // CMAX
    cell_count = cluster_count * CMAX
    owner_of = cluster // cluster_count
    owner_hit = (owner_of[:, None] == lax.broadcasted_iota(jnp.int32, (1, owner_count), 1)).astype(
        jnp.int32
    )
    within_pair = jnp.sum((jnp.cumsum(owner_hit, axis=0) - owner_hit) * owner_hit, axis=1)
    target = owner_of * slot_rows + within_pair
    coords = jnp.stack([cluster % cluster_count, cluster_rank], axis=1).astype(jnp.float32)
    vacant = jnp.concatenate(
        [
            jnp.full((owner_count * slot_rows, 1), cluster_count, jnp.float32),
            jnp.zeros((owner_count * slot_rows, 1), jnp.float32),
        ],
        axis=1,
    )
    labels = vacant.at[target].set(coords).astype(jnp.bfloat16).reshape(owner_count, 2 * slot_rows)
    whitened = whiten(values, inverse_root, average)
    outgoing = (
        jnp.zeros((owner_count * slot_rows, feat_dim), jnp.bfloat16)
        .at[target]
        .set(whitened)
        .reshape(owner_count, slot_rows, feat_dim)
    )
    arrived, labels_in = (
        lax.all_to_all(outgoing, "grp", split_axis=0, concat_axis=0, tiled=True),
        lax.all_to_all(labels, "grp", split_axis=0, concat_axis=0, tiled=True),
    )
    units_in = arrived.reshape(owner_count * slot_rows, feat_dim)
    placed = labels_in.reshape(owner_count * slot_rows, 2).astype(jnp.int32)
    cell_index = placed[:, 0] * CMAX + placed[:, 1]
    table = (
        jnp.zeros((cell_count, feat_dim), jnp.bfloat16).at[cell_index].set(units_in, mode="drop")
    )
    occupied = jnp.zeros((cell_count,), jnp.int32).at[cell_index].set(1, mode="drop") > 0
    highest = best_within(table, occupied, cluster_count)
    answer = highest[jnp.minimum(cell_index, cell_count - 1)].reshape(owner_count, slot_rows)
    returned = lax.all_to_all(answer, "grp", split_axis=0, concat_axis=0, tiled=True)
    return returned.reshape(owner_count * slot_rows)[target]


def solution(mesh):
    placed = (
        P(("grp", "rep"), None),
        P(("grp", "rep"), None),
        P(("grp", "rep")),
        P(("grp", "rep")),
    )
    return jax.shard_map(
        local, mesh=mesh, in_specs=placed, out_specs=P(("grp", "rep")), check_vma=False
    )
```

profile of v0, /device:TPU:2, one launch (start us, length us, event | category | flops | bytes accessed | tf_op | source)
XLA Modules:
  0.0 647.7 jit_solution(15239859383687438242)
XLA Ops:
  11.9 78.8 %psum.15 = f32[1024]{0:T(1024)S(1)} all-reduce(f32[1024]{0:T(1024)S(1)} %get-tuple-element.9), channel_id=1, replica_groups=mesh['grp'=64,'rep'=4] {'grp','rep'}, use_global_device_ids=true, to_apply=%region_7.8 | all-reduce | flops 1024 | bytes 8192 | tf_op jit(solution)/shard_map/psum | solution.py:74
  90.7 195.7 %all-reduce.2.cloned.1.call-done = f32[1024,1024]{1,0:T(8,128)} async-done(((f32[1024,1024]{1,0:T(8,128)}), f32[1024,1024]{1,0:T(8,128)}) %all-reduce.2.cloned.1.call-update) | async-done | bytes 4194320 | tf_op jit(solution)/shard_map/psum | solution.py:74
  286.3 4.2 multiply_reduce_fusion
  294.8 3.8 fusion.14
  298.6 3.8 fusion.33
  302.5 4.8 fusion.4
  307.4 47.3 %all-gather.5.cloned.1.call-done = f32[1024,1024]{1,0:T(8,128)} async-done(((f32[256,1024]{1,0:T(8,128)}), f32[1024,1024]{1,0:T(8,128)}) %all-gather.5.cloned.1.call-update) | async-done | bytes 4194320 | tf_op jit(solution)/shard_map/all_gather | solution.py:91
  354.6 6.3 fusion.12
  361.0 3.7 fusion.37
  364.7 4.8 fusion.3
  369.6 50.1 %all-gather.7.cloned.1.call-done = f32[1024,1024]{1,0:T(8,128)} async-done(((f32[256,1024]{1,0:T(8,128)}), f32[1024,1024]{1,0:T(8,128)}) %all-gather.7.cloned.1.call-update) | async-done | bytes 4194320 | tf_op jit(solution)/shard_map/all_gather | solution.py:91
  419.7 6.6 %fusion.10 = f32[256,1024]{1,0:T(8,128)S(1)} fusion(f32[1024,1024]{1,0:T(8,128)} %all-gather.7.cloned.1.call-done, f32[1024,1024]{1,0:T(8,128)} %copy-done.3, s32[]{:T(128)S(6)} %select_n.38), kind=kOutput, calls=%fused_computation.32 | convolution fusion | flops 3221225472 | bytes 6291460 | tf_op jit(solution)/shard_map/dot_general | solution.py:42
  430.1 4.8 fusion.2
  434.9 50.1 %all-gather.9.cloned.1.call-done = f32[1024,1024]{1,0:T(8,128)} async-done(((f32[256,1024]{1,0:T(8,128)}), f32[1024,1024]{1,0:T(8,128)}) %all-gather.9.cloned.1.call-update) | async-done | bytes 4194320 | tf_op jit(solution)/shard_map/all_gather | solution.py:91
  485.0 6.3 fusion.8
  491.3 3.7 fusion.39
  495.1 4.6 fusion.5
  503.0 13.0 %all-to-all-start = ((bf16[64,1,24]{2,1,0:T(2,128)(2,1)}), bf16[64,1,24]{2,1,0:T(2,128)(2,1)S(1)}, u32[]{:S(2)}, u32[]{:S(2)}) async-start(bf16[64,1,24]{2,1,0:T(2,128)(2,1)} %all_to_all.20), calls=%async_computation | async-start | bytes 65536 | tf_op jit(solution)/shard_map/all_to_all | solution.py:122
  516.0 17.1 %all-gather.11.cloned.1.call-done = bf16[1024,1024]{1,0:T(8,128)(2,1)} async-done(((bf16[256,1024]{1,0:T(8,128)(2,1)}), bf16[1024,1024]{1,0:T(8,128)(2,1)}) %all-gather.11.cloned.1.call-update) | async-done | bytes 2097168 | tf_op jit(solution)/shard_map/all_gather | solution.py:93
  541.8 12.7 %all-to-all-start.1 = ((bf16[64,12,1024]{2,1,0:T(8,128)(2,1)}), bf16[64,12,1024]{2,1,0:T(8,128)(2,1)S(1)}, u32[]{:S(2)}, u32[]{:S(2)}) async-start(bf16[64,12,1024]{2,1,0:T(8,128)(2,1)} %reshape.72), calls=%async_computation.1 | async-start | bytes 4194304 | tf_op jit(solution)/shard_map/all_to_all | solution.py:121
  558.7 46.9 %all-to-all-done.1 = bf16[64,12,1024]{2,1,0:T(8,128)(2,1)S(1)} async-done(((bf16[64,12,1024]{2,1,0:T(8,128)(2,1)}), bf16[64,12,1024]{2,1,0:T(8,128)(2,1)S(1)}, u32[]{:S(2)}, u32[]{:S(2)}) %all-to-all-start.1) | async-done | bytes 1572896 | tf_op jit(solution)/shard_map/all_to_all | solution.py:121
  607.0 6.8 %scatter_custom_fusion.3 = bf16[768,1024]{1,0:T(8,128)(2,1)S(1)} fusion(s32[768]{0:T(1024)S(1)} %get-tuple-element.6, bf16[768,1024]{1,0:T(8,128)(2,1)} %reshape.121, bf16[]{:T(256)} %constant.27.clone.1), kind=kCustom, calls=%fused_computation.38 | custom fusion | bytes 1573376 | tf_op jit(solution)/shard_map/scatter | solution.py:128
  618.3 8.4 %all-to-all-start.2 = ((f32[64,1,12]{2,1,0:T(1,128)}), f32[64,1,12]{2,1,0:T(1,128)S(1)}, u32[]{:S(2)}, u32[]{:S(2)}) async-start(f32[64,1,12]{2,1,0:T(1,128)} %bitcast.7), calls=%async_computation.2 | async-start | bytes 65536 | tf_op jit(solution)/shard_map/all_to_all | solution.py:133
  626.7 10.9 %all-to-all-done.2 = f32[64,1,12]{2,1,0:T(1,128)S(1)} async-done(((f32[64,1,12]{2,1,0:T(1,128)}), f32[64,1,12]{2,1,0:T(1,128)S(1)}, u32[]{:S(2)}, u32[]{:S(2)}) %all-to-all-start.2) | async-done | bytes 3104 | tf_op jit(solution)/shard_map/all_to_all | solution.py:133
  (76 shorter events, 38.0 us)
Async XLA Ops:
  6.5 279.8 %all-reduce.2.cloned.1.call-start = ((), (), s32[]{:S(2)}) async-start(), calls=%async_computation.3 | async-start | bytes 8388608 | tf_op jit(solution)/shard_map/psum | solution.py:74
  11.8 342.8 %all-gather.5.cloned.1.call-start = ((), (), s32[]{:S(2)}) async-start(), calls=%async_computation.4 | async-start | bytes 5242880 | tf_op jit(solution)/shard_map/all_gather | solution.py:91
  294.8 7.7 %copy-start.3 = (f32[1024,1024]{1,0:T(8,128)}, f32[1024,1024]{1,0:T(8,128)S(1)}, u32[]{:S(2)}) copy-start(f32[1024,1024]{1,0:T(8,128)S(1)} %get-tuple-element.8) | copy-start | bytes 12582916
  307.3 112.4 %all-gather.7.cloned.1.call-start = ((), (), s32[]{:S(2)}) async-start(), calls=%async_computation.5 | async-start | bytes 5242880 | tf_op jit(solution)/shard_map/all_gather | solution.py:91
  354.6 6.3 copy-start
  361.0 3.7 copy-start.5
  369.6 115.4 %all-gather.9.cloned.1.call-start = ((), (), s32[]{:S(2)}) async-start(), calls=%async_computation.6 | async-start | bytes 5242880 | tf_op jit(solution)/shard_map/all_gather | solution.py:91
  419.7 6.6 %copy-start.1 = (f32[1024,1024]{1,0:T(8,128)S(1)}, f32[1024,1024]{1,0:T(8,128)}, u32[]{:S(2)}) copy-start(f32[1024,1024]{1,0:T(8,128)} %all-gather.7.cloned.1.call-done) | copy-start | bytes 12582916
  426.3 3.7 copy-start.4
  434.9 98.2 %all-gather.11.cloned.1.call-start = ((), (), s32[]{:S(2)}) async-start(), calls=%async_computation.7 | async-start | bytes 2621440 | tf_op jit(solution)/shard_map/all_gather | solution.py:93
  485.0 6.3 copy-start.2
  491.3 3.8 copy-start.6
  495.1 4.6 copy-start.8
  495.1 5.5 copy-start.9
  495.1 5.8 copy-start.7
  503.0 38.8 %all-to-all-start = ((bf16[64,1,24]{2,1,0:T(2,128)(2,1)}), bf16[64,1,24]{2,1,0:T(2,128)(2,1)S(1)}, u32[]{:S(2)}, u32[]{:S(2)}) async-start(bf16[64,1,24]{2,1,0:T(2,128)(2,1)} %all_to_all.20), calls=%async_computation | async-start | bytes 65536 | tf_op jit(solution)/shard_map/all_to_all | solution.py:122
  541.8 63.9 %all-to-all-start.1 = ((bf16[64,12,1024]{2,1,0:T(8,128)(2,1)}), bf16[64,12,1024]{2,1,0:T(8,128)(2,1)S(1)}, u32[]{:S(2)}, u32[]{:S(2)}) async-start(bf16[64,12,1024]{2,1,0:T(8,128)(2,1)} %reshape.72), calls=%async_computation.1 | async-start | bytes 4194304 | tf_op jit(solution)/shard_map/all_to_all | solution.py:121
  618.3 19.3 %all-to-all-start.2 = ((f32[64,1,12]{2,1,0:T(1,128)}), f32[64,1,12]{2,1,0:T(1,128)S(1)}, u32[]{:S(2)}, u32[]{:S(2)}) async-start(f32[64,1,12]{2,1,0:T(1,128)} %bitcast.7), calls=%async_computation.2 | async-start | bytes 65536 | tf_op jit(solution)/shard_map/all_to_all | solution.py:133
Sparse Core Ops, SparseCore 0:
  12.8 273.4 all-reduce.1
  307.4 47.1 all-gather.4
  369.7 49.9 all-gather.6
  435.0 49.9 all-gather.8
  499.8 33.2 all-gather.10
where the time goes:
time: 652 us; the launch traced here: 648 us
  waiting for transfers between devices  418 us (64%)
  blocking collectives  78.8 us (12%)
  matrix products  65.2 us (10%)
  starting transfers between devices  34.2 us (5%)
  local copies, waits for them, and re-layouts  23.4 us (4%)
  between operations  14.5 us (2%)
  other arithmetic  13.4 us (2%)
    psum x1, waiting for transfers between devices, local(): lax.psum((lax.dot_general(values, values, (((0,), (0,)), ((), ())), prefe...  196 us
    all_gather x3, waiting for transfers between devices, local(): lax.all_gather(slab_rows, 'rep', axis=0, tiled=True)  147 us
    psum x1, blocking collectives, local(): lax.psum((lax.dot_general(values, values, (((0,), (0,)), ((), ())), prefe...  78.8 us
    all_to_all x1, waiting for transfers between devices, local(): lax.all_to_all(outgoing, 'grp', split_axis=0, concat_axis=0, tiled=True)  46.9 us
    dot_general x8, matrix products, newton_rows(): product = jnp.dot(product, whole, precision=EXACT_MODE)  34 us
    dot_general x4, matrix products, newton_rows(): product = jnp.dot(normed_rows, whole, precision=EXACT_MODE)  23 us
    all_gather x1, waiting for transfers between devices, local(): lax.all_gather(final_rows.astype(jnp.bfloat16), 'rep', axis=0, tiled=True)  17.1 us
  transfers between devices with their start and end apart: 8, of which 7 were waited for; matrix products, arithmetic and copies ran while one was open for 2% of the time, Pallas kernels for 0%

commit v1 on v0

v1 whole, which is shorter than its diff:
```python
import jax
import jax.numpy as jnp
from jax import lax
from jax.experimental import pallas as pl
from jax.experimental.pallas import tpu as pltpu
from jax.sharding import PartitionSpec as P

MESH = pl.DeviceIdType.MESH
F32 = jnp.float32
BF16 = jnp.bfloat16

D = 1024
BLK = 128
ROWS = 256
ROW_TOTAL = 65536
NG = 64
CPO = 12
SLOT = 16
NROW = NG * SLOT
LABEL = 12
COV_EPS = 0.001
UNIT_EPS = 1e-06

SIZE = {"x": 4, "y": 4, "z": 8}
COLOURS = (("xyz", 1152), ("yzx", 768), ("zxy", 512))
HALF = sum(rows for _, rows in COLOURS)
BASES = (0, 1152, 1920)
SUMS = 36 * BLK
MB = 256
NB = D // MB


def block_row(i, j):
    return (i * 8 - (i * (i - 1)) // 2 + (j - i)) * BLK


def aligned(v, m=8):
    return pl.multiple_of(v, m)


def split(v):
    hi = v.astype(BF16)
    return hi, (v - hi.astype(F32)).astype(BF16)


def thirds(v):
    a = v.astype(BF16)
    rest = v - a.astype(F32)
    b = rest.astype(BF16)
    return a, b, (rest - b.astype(F32)).astype(BF16)


def inverse_sqrt(v):
    y = lax.rsqrt(v)
    y = y * (1.5 - 0.5 * (v * y) * y)
    return y * (1.5 - 0.5 * (v * y) * y)


def nn(a, b):
    return jnp.dot(a, b, preferred_element_type=F32)


def nt(a, b):
    return lax.dot_general(a, b, (((1,), (1,)), ((), ())), preferred_element_type=F32)


def tn(a, b):
    return lax.dot_general(a, b, (((0,), (0,)), ((), ())), preferred_element_type=F32)


def iota(shape, dim):
    return lax.broadcasted_iota(jnp.int32, shape, dim)


def kernel(emb, sca, clu, out, vals, tri, tot, buf0, buf1, buf2, buf3, disp, arr, ret, got,
           nh, nl, wh, mh, ml, ah, al, eh, qh, ql, zh, zl, th, tl, kh, kl, lin, acc, avg8, off,
           send_sem, recv_sem, a2a_send, a2a_recv):
    g = lax.axis_index("grp")
    r = lax.axis_index("rep")
    core = r % 2
    me = {"x": g % 4, "y": ((g // 4) % 2) * 2 + r // 2, "z": g // 8}

    def device(x, y, z, c):
        return (z * 8 + (y // 2) * 4 + x, (y % 2) * 2 + c)

    def peer(axis, d):
        at = dict(me)
        at[axis] = (me[axis] + d) % SIZE[axis]
        return device(at["x"], at["y"], at["z"], core)

    partner = (g, r + 1 - 2 * core)

    barrier = pltpu.get_barrier_semaphore()

    def greet(d, carry):
        pl.semaphore_signal(barrier, inc=1, device_id=((g + d) % NG, r), device_id_type=MESH)
        return carry

    lax.fori_loop(1, NG, greet, 0)
    for d in (1, 2, 3):
        pl.semaphore_signal(barrier, inc=1, device_id=peer("y", d), device_id_type=MESH)
    pl.semaphore_signal(barrier, inc=1, device_id=partner, device_id_type=MESH)

    for b in range(8):
        cols = slice(b * BLK, (b + 1) * BLK)
        v = (emb[:, cols].astype(F32) * sca[:, b:b + 1]).astype(BF16)
        vals[:, cols] = v
        tri[SUMS + b:SUMS + b + 1, :] = jnp.sum(v.astype(F32), axis=0, keepdims=True)
    tri[SUMS + 8:SUMS + 2 * BLK, :] = jnp.zeros((2 * BLK - 8, BLK), F32)
    for i in range(8):
        panel = tn(vals[:, i * BLK:(i + 1) * BLK], vals[:, i * BLK:])
        for j in range(i, 8):
            row = block_row(i, j)
            tri[row:row + BLK, :] = panel[:, (j - i) * BLK:(j - i + 1) * BLK]

    pl.semaphore_wait(barrier, NG - 1 + 3 + 1)

    sem_at = [0]

    def copies(todo):
        started = []
        for src, dst, to, slot in todo:
            desc = pltpu.make_async_remote_copy(
                src_ref=src, dst_ref=dst, send_sem=send_sem.at[slot], recv_sem=recv_sem.at[slot],
                device_id=to, device_id_type=MESH)
            desc.start()
            started.append(desc)
        return started

    every = []

    def launch(todo):
        started = copies(todo)
        every.extend(started)
        return started

    def fresh(n):
        first = sem_at[0]
        sem_at[0] += n
        return first

    mine = core * HALF
    other = HALF - mine
    pending = []
    for c, (axes, rows) in enumerate(COLOURS):
        s = fresh(1)
        pending.append(launch([(
            tri.at[pl.ds(aligned(other + BASES[c]), rows)], buf0.at[pl.ds(BASES[c], rows)], partner, s)]))

    cl_row = clu[...].astype(F32)
    cl_b = jnp.broadcast_to(cl_row, (ROWS, ROWS))
    cl_t = cl_b.T
    own_b = jnp.floor((cl_b + 0.5) * (1.0 / CPO))
    own_t = jnp.floor((cl_t + 0.5) * (1.0 / CPO))
    same = own_b == own_t
    si = iota((ROWS, ROWS), 0)
    li = iota((ROWS, ROWS), 1)
    slot_row = jnp.sum(jnp.where(same & (si < li), 1.0, 0.0), axis=0, keepdims=True)
    slot_col = jnp.sum(jnp.where(same & (li < si), 1.0, 0.0), axis=1, keepdims=True)
    own_row = own_b[0:1, :]
    label_at = slot_col * 16.0 + (cl_t[:, 0:1] - CPO * own_t[:, 0:1])
    labels = jnp.where(li.astype(F32) == label_at, 1.0, 0.0).astype(BF16)
    target = own_row * SLOT + slot_row
    label_row = own_row * SLOT + LABEL
    for k in range(4):
        rows = iota((256, ROWS), 0).astype(F32) + (k * 256.0)
        pick = jnp.where(rows == target, 1.0, 0.0).astype(BF16)
        pick_label = jnp.where(rows == label_row, 1.0, 0.0).astype(BF16)
        sorted_rows = nn(pick, vals[...])
        disp[k * 256:(k + 1) * 256, 256:] = sorted_rows[:, 256:].astype(BF16)
        disp[k * 256:(k + 1) * 256, 0:256] = (sorted_rows[:, 0:256] + nn(pick_label, labels)).astype(BF16)

    bases, sizes = [], []
    step1, step2, step3 = [], [], []
    for c, (axes, rows) in enumerate(COLOURS):
        for desc in pending[c]:
            desc.wait_recv()
        base = aligned(mine + BASES[c])
        tri[pl.ds(base, rows), :] += buf0[BASES[c]:BASES[c] + rows, :]
        n = SIZE[axes[0]]
        part = rows // n
        s = fresh(n - 1)
        step1.append(launch([(
            tri.at[pl.ds(aligned(base + ((me[axes[0]] + d) % n) * part), part)],
            buf1.at[pl.ds(BASES[c] + (n - 1 - d) * part, part)], peer(axes[0], d), s + n - 1 - d)
            for d in range(1, n)]))
    for c, (axes, rows) in enumerate(COLOURS):
        for desc in step1[c]:
            desc.wait_recv()
        n = SIZE[axes[0]]
        part = rows // n
        base = aligned(mine + BASES[c] + me[axes[0]] * part)
        total = tri[pl.ds(base, part), :]
        for k in range(n - 1):
            total = total + buf1[BASES[c] + k * part:BASES[c] + (k + 1) * part, :]
        tri[pl.ds(base, part), :] = total
        n2 = SIZE[axes[1]]
        part2 = part // n2
        s = fresh(n2 - 1)
        step2.append(launch([(
            tri.at[pl.ds(aligned(base + ((me[axes[1]] + d) % n2) * part2), part2)],
            buf2.at[c, pl.ds((n2 - 1 - d) * part2, part2)], peer(axes[1], d), s + n2 - 1 - d)
            for d in range(1, n2)]))
    for c, (axes, rows) in enumerate(COLOURS):
        for desc in step2[c]:
            desc.wait_recv()
        part = rows // SIZE[axes[0]]
        n2 = SIZE[axes[1]]
        part2 = part // n2
        base = aligned(mine + BASES[c] + me[axes[0]] * part + me[axes[1]] * part2)
        total = tri[pl.ds(base, part2), :]
        for k in range(n2 - 1):
            total = total + buf2[c, k * part2:(k + 1) * part2, :]
        tri[pl.ds(base, part2), :] = total
        n3 = SIZE[axes[2]]
        s = fresh(n3 - 1)
        step3.append(launch([(
            tri.at[pl.ds(base, part2)], buf3.at[c, pl.ds((n3 - 1 - d) * part2, part2)],
            peer(axes[2], d), s + n3 - 1 - d) for d in range(1, n3)]))
    gather2, gather1, gather0 = [], [], []
    for c, (axes, rows) in enumerate(COLOURS):
        for desc in step3[c]:
            desc.wait_recv()
        n2, n3 = SIZE[axes[1]], SIZE[axes[2]]
        part = rows // SIZE[axes[0]]
        part2 = part // n2
        base = aligned(mine + BASES[c] + me[axes[0]] * part + me[axes[1]] * part2)
        total = tri[pl.ds(base, part2), :]
        for k in range(n3 - 1):
            total = total + buf3[c, k * part2:(k + 1) * part2, :]
        tot[pl.ds(base, part2), :] = total
        s = fresh(n2 - 1)
        gather2.append(launch([(
            tot.at[pl.ds(base, part2)], tot.at[pl.ds(base, part2)], peer(axes[1], d), s + n2 - 1 - d)
            for d in range(1, n2)]))
    for c, (axes, rows) in enumerate(COLOURS):
        for desc in gather2[c]:
            desc.wait_recv()
        n = SIZE[axes[0]]
        part = rows // n
        base = aligned(mine + BASES[c] + me[axes[0]] * part)
        s = fresh(n - 1)
        gather1.append(launch([(
            tot.at[pl.ds(base, part)], tot.at[pl.ds(base, part)], peer(axes[0], d), s + n - 1 - d)
            for d in range(1, n)]))
    for c, (axes, rows) in enumerate(COLOURS):
        for desc in gather1[c]:
            desc.wait_recv()
        base = aligned(mine + BASES[c])
        s = fresh(1)
        gather0.append(launch([(tot.at[pl.ds(base, rows)], tot.at[pl.ds(base, rows)], partner, s)]))

    def post(d, carry):
        to = (g + d) % NG
        pltpu.make_async_remote_copy(
            src_ref=disp.at[pl.ds(aligned(to * SLOT, SLOT), SLOT)],
            dst_ref=arr.at[pl.ds(aligned(g * SLOT, SLOT), SLOT)],
            send_sem=a2a_send.at[0], recv_sem=a2a_recv.at[0],
            device_id=(to, r), device_id_type=MESH).start()
        return carry

    lax.fori_loop(1, NG, post, 0)
    arr[pl.ds(aligned(g * SLOT, SLOT), SLOT), :] = disp[pl.ds(aligned(g * SLOT, SLOT), SLOT), :]

    for c in range(3):
        for desc in gather0[c]:
            desc.wait_recv()

    inv_n = 1.0 / ROW_TOTAL
    acc[...] = jnp.zeros_like(acc)
    eye = jnp.where(iota((BLK, BLK), 0) == iota((BLK, BLK), 1), COV_EPS, 0.0)
    for i in range(8):
        mean_i = jnp.broadcast_to(tot[SUMS + i:SUMS + i + 1, :] * inv_n, (BLK, BLK))
        avg8[:, i * BLK:(i + 1) * BLK] = mean_i[0:8, :]
        mean_col = mean_i.T
        row = block_row(i, i)
        cov = tot[row:row + BLK, :] * inv_n - mean_col * mean_i + eye
        lin[i * BLK:(i + 1) * BLK, i * BLK:(i + 1) * BLK] = cov
        acc[...] += cov * cov

        def centre(j, carry, i=i, mean_col=mean_col):
            at = pl.ds(aligned((i * 8 - (i * (i - 1)) // 2 + (j - i)) * BLK, BLK), BLK)
            mean_j = tot[pl.ds(SUMS + j, 1), :] * inv_n
            cov = tot[at, :] * inv_n - mean_col * mean_j
            lin[i * BLK:(i + 1) * BLK, pl.ds(aligned(j * BLK, BLK), BLK)] = cov
            acc[...] += 2.0 * (cov * cov)
            return carry

        if i < 7:
            lax.fori_loop(i + 1, 8, centre, 0)
    squares = jnp.sum(jnp.sum(acc[...], axis=1, keepdims=True), axis=0, keepdims=True)
    scale = inverse_sqrt(squares)
    for i in range(8):
        def place(j, carry, i=i):
            v = lin[i * BLK:(i + 1) * BLK, pl.ds(aligned(j * BLK, BLK), BLK)] * scale
            hi, lo = split(v)
            vt = v.T
            hi_t, lo_t = split(vt)
            there = pl.ds(aligned(j * BLK, BLK), BLK)
            nh[there, i * BLK:(i + 1) * BLK] = hi_t
            nl[there, i * BLK:(i + 1) * BLK] = lo_t
            nh[i * BLK:(i + 1) * BLK, there] = hi
            nl[i * BLK:(i + 1) * BLK, there] = lo
            return carry

        lax.fori_loop(i, 8, place, 0)

    def product(terms, finish):
        def row(i, carry):
            def cell(j, carry):
                ri = pl.ds(aligned(i * MB, MB), MB)
                cj = pl.ds(aligned(j * MB, MB), MB)
                v = None
                for a, b in terms:
                    p = nn(a[ri, :], b[:, cj])
                    v = p if v is None else v + p
                finish(v, i, j, ri, cj)
                return carry
            lax.fori_loop(i, NB, cell, 0)
            return carry
        lax.fori_loop(0, NB, row, 0)

    def put(ref, v, ri, cj):
        ref[cj, ri] = v.T.astype(BF16)
        ref[ri, cj] = v.astype(BF16)

    def put2(hi_ref, lo_ref, v, ri, cj, both=False):
        hi, lo = split(v)
        vt = v.T
        if both:
            hi_t, lo_t = split(vt)
            hi_ref[cj, ri] = hi_t
            lo_ref[cj, ri] = lo_t
        else:
            hi_ref[cj, ri] = vt.astype(BF16)
        hi_ref[ri, cj] = hi
        lo_ref[ri, cj] = lo

    def read(hi_ref, lo_ref, ri, cj):
        return hi_ref[ri, cj].astype(F32) + lo_ref[ri, cj].astype(F32)

    def step_w(v, i, j, ri, cj):
        put(wh, 0.25 * v - 1.5 * read(nh, nl, ri, cj), ri, cj)

    product([(nh, nh)], step_w)

    def step_m(v, i, j, ri, cj):
        put2(mh, ml, v + 2.25 * read(nh, nl, ri, cj), ri, cj)

    product([(nh, wh)], step_m)

    def square(m_hi, m_lo, keep_lo):
        def run(v, i, j, ri, cj):
            m = read(m_hi, m_lo, ri, cj)
            put(eh, 1.125 * m - 0.125 * v, ri, cj)
            if keep_lo:
                put2(ah, al, v, ri, cj, both=True)
            else:
                put(ah, v, ri, cj)
            lin[ri, cj] = 1.6875 * v - 2.4375 * m
        return run

    product([(mh, mh)], square(mh, ml, False))

    def step_q(v, i, j, ri, cj):
        put2(qh, ql, lin[ri, cj] - 0.5 * v, ri, cj)

    product([(ah, eh)], step_q)

    def step_z(v, i, j, ri, cj):
        put2(zh, zl, 1.5 * read(qh, ql, ri, cj) - 1.125 * read(nh, nl, ri, cj) - 0.5 * v, ri, cj)

    product([(nh, qh)], step_z)

    def step_t(v, i, j, ri, cj):
        put2(th, tl, 2.25 * read(mh, ml, ri, cj) + v, ri, cj)

    product([(mh, qh)], step_t)

    def step_k(v, i, j, ri, cj):
        put2(kh, kl, 2.25 * read(th, tl, ri, cj) + v, ri, cj, both=True)

    product([(th, qh)], step_k)
    product([(kh, kh), (kh, kl), (kl, kh)], square(kh, kl, True))

    def step_q3(v, i, j, ri, cj):
        q = lin[ri, cj] - 0.5 * v
        put(qh, q, ri, cj)
        diag = jnp.where(iota((MB, MB), 0) + i * MB == iota((MB, MB), 1) + j * MB, 3.375 * 2.25, 0.0)
        lin[ri, cj] = 3.375 * q + diag + 2.25 * read(zh, zl, ri, cj)

    product([(ah, eh), (al, eh)], step_q3)

    def step_root(v, i, j, ri, cj):
        put(wh, lin[ri, cj] + v, ri, cj)

    product([(zh, qh)], step_root)

    sub = iota((8, D), 0)
    a0, a1, a2 = thirds(avg8[...])
    mean8 = jnp.where(sub == 0, a0.astype(F32),
                      jnp.where(sub == 1, a1.astype(F32), jnp.where(sub == 2, a2.astype(F32), 0.0)))
    off[...] = jnp.sum(nn(mean8.astype(BF16), wh[...]), axis=0, keepdims=True)

    pltpu.make_async_copy(arr.at[pl.ds(0, NROW - SLOT)], arr.at[pl.ds(0, NROW - SLOT)], a2a_recv.at[0]).wait()

    pick12 = jnp.where(iota((NG, NROW), 1) == iota((NG, NROW), 0) * SLOT + LABEL, 1.0, 0.0).astype(BF16)
    lab = nn(pick12, arr[:, 0:256]).astype(BF16)
    spread = jnp.where(iota((NROW, NG), 0) // SLOT == iota((NROW, NG), 1), 1.0, 0.0).astype(BF16)
    fold = jnp.where(iota((256, BLK), 0) % 16 == iota((256, BLK), 1), 1.0, 0.0).astype(BF16)
    full = nn(spread, lab)
    full = jnp.where(iota((NROW, 256), 1) // 16 == iota((NROW, 256), 0) % SLOT, full, 0.0).astype(BF16)
    member = nn(full, fold).astype(BF16)

    def whiten(i, carry):
        ri = pl.ds(aligned(i * MB, MB), MB)
        p = nn(arr[ri, :], wh[...]) - off[...]
        energy = jnp.sum(p * p, axis=1, keepdims=True)
        eh[ri, :] = (p * inverse_sqrt(energy + UNIT_EPS)).astype(BF16)
        return carry

    lax.fori_loop(0, NB, whiten, 0)
    ah[:, 0:BLK] = member

    def compare(i, carry):
        ri = pl.ds(aligned(i * MB, MB), MB)
        s = nt(eh[ri, :], eh[...])
        together = nt(ah[ri, 0:BLK], ah[:, 0:BLK])
        distinct = iota((MB, NROW), 0) + i * MB != iota((MB, NROW), 1)
        best = jnp.max(jnp.where((together > 0.5) & distinct, s, -1.0), axis=1, keepdims=True)
        best = jnp.maximum(best, -1.0)
        spot = iota((MB, BLK), 1) == iota((MB, BLK), 0) % SLOT
        lanes = jnp.where(spot, jnp.broadcast_to(best, (MB, BLK)), 0.0)
        ret[pl.ds(i * (MB // SLOT), MB // SLOT)] = jnp.sum(
            lanes.reshape(MB // SLOT, SLOT, BLK), axis=1, keepdims=True)
        return carry

    lax.fori_loop(0, NB, compare, 0)

    def answer(d, carry):
        to = (g + d) % NG
        pltpu.make_async_remote_copy(
            src_ref=ret.at[to], dst_ref=got.at[g], send_sem=a2a_send.at[1], recv_sem=a2a_recv.at[1],
            device_id=(to, r), device_id_type=MESH).start()
        return carry

    lax.fori_loop(1, NG, answer, 0)
    got[g] = ret[g]
    pltpu.make_async_copy(got.at[pl.ds(0, NG - 1)], got.at[pl.ds(0, NG - 1)], a2a_recv.at[1]).wait()

    rows = got[...].reshape(NG, BLK)
    owner_pick = jnp.where(iota((NG, ROWS), 0).astype(F32) == own_row, 1.0, 0.0).astype(BF16)
    picked = jnp.zeros((BLK, ROWS), F32)
    for part in thirds(rows.T):
        picked = picked + nn(part, owner_pick)
    hit = iota((BLK, ROWS), 0).astype(F32) == slot_row
    out[...] = jnp.sum(jnp.where(hit, picked, 0.0), axis=0, keepdims=True)

    for desc in every:
        desc.wait_send()
    pltpu.make_async_copy(disp.at[pl.ds(0, NROW - SLOT)], disp.at[pl.ds(0, NROW - SLOT)], a2a_send.at[0]).wait()
    pltpu.make_async_copy(ret.at[pl.ds(0, NG - 1)], ret.at[pl.ds(0, NG - 1)], a2a_send.at[1]).wait()


def sem_count():
    n = 0
    for axes, _ in COLOURS:
        a, b, c = (SIZE[k] - 1 for k in axes)
        n += 2 + 2 * a + 2 * b + c
    return n


def local(embeddings, scales, cluster, cluster_rank):
    vm = lambda shape, dtype: pltpu.VMEM(shape, dtype)
    mat = lambda: pltpu.VMEM((D, D), BF16)
    part2 = [rows // SIZE[a[0]] // SIZE[a[1]] for a, rows in COLOURS]
    scratch = [
        vm((ROWS, D), BF16),
        vm((2 * HALF, BLK), F32),
        vm((2 * HALF, BLK), F32),
        vm((HALF, BLK), F32),
        vm((HALF, BLK), F32),
        vm((3, max((SIZE[a[1]] - 1) * p for (a, _), p in zip(COLOURS, part2)), BLK), F32),
        vm((3, max((SIZE[a[2]] - 1) * p for (a, _), p in zip(COLOURS, part2)), BLK), F32),
        vm((NROW, D), BF16),
        vm((NROW, D), BF16),
        vm((NG, 1, BLK), F32),
        vm((NG, 1, BLK), F32),
    ] + [mat() for _ in range(16)] + [
        vm((D, D), F32),
        vm((BLK, BLK), F32),
        vm((8, D), F32),
        vm((1, D), F32),
        pltpu.SemaphoreType.DMA((sem_count(),)),
        pltpu.SemaphoreType.DMA((sem_count(),)),
        pltpu.SemaphoreType.DMA((2,)),
        pltpu.SemaphoreType.DMA((2,)),
    ]
    vmem = pl.BlockSpec(memory_space=pltpu.VMEM)
    best = pl.pallas_call(
        kernel,
        out_shape=jax.ShapeDtypeStruct((1, ROWS), F32),
        in_specs=[vmem, vmem, vmem],
        out_specs=vmem,
        scratch_shapes=scratch,
        compiler_params=pltpu.CompilerParams(
            collective_id=0, has_side_effects=True, vmem_limit_bytes=67043328),
    )(embeddings, scales, cluster.reshape(1, ROWS))
    return best.reshape(ROWS)


def solution(mesh):
    placed = (
        P(("grp", "rep"), None),
        P(("grp", "rep"), None),
        P(("grp", "rep")),
        P(("grp", "rep")),
    )
    return jax.shard_map(
        local, mesh=mesh, in_specs=placed, out_specs=P(("grp", "rep")), check_vma=False
    )
```

time: 652 us -> 126 us (0.19)
  waiting for transfers between devices: 418 us -> 0 us
  Pallas kernels: 0 us -> 122 us
  blocking collectives: 78.8 us -> 0 us
  matrix products: 65.2 us -> 0 us
  starting transfers between devices: 34.2 us -> 0 us
  local copies, waits for them, and re-layouts: 23.4 us -> 2.7 us
  between operations: 14.5 us -> 0.02 us
  other arithmetic: 13.4 us -> 0 us
    psum x1 -> x0, waiting for transfers between devices: 196 us -> none  [local(): lax.psum((lax.dot_general(values, values, (((0,), (0,)), ((), ())), prefe...]
    all_gather x4 -> x0, waiting for transfers between devices: 164 us -> none  [the longest x3 147 us: local(): lax.all_gather(slab_rows, 'rep', axis=0, tiled=True)]
    pallas_call x0 -> x1, Pallas kernels: none -> 122 us  [local(): pl.pallas_call(kernel, out_shape=jax.ShapeDtypeStruct((1, ROWS), F32), in...]
    psum x1 -> x0, blocking collectives: 78.8 us -> none  [local(): lax.psum((lax.dot_general(values, values, (((0,), (0,)), ((), ())), prefe...]
    dot_general x16 -> x0, matrix products: 65.2 us -> none  [the longest x8 34 us: newton_rows(): product = jnp.dot(product, whole, precision=EXACT_MODE)]
    all_to_all x3 -> x0, waiting for transfers between devices: 57.9 us -> none  [the longest x1 46.9 us: local(): lax.all_to_all(outgoing, 'grp', split_axis=0, concat_axis=0, tiled=True)]
    all_to_all x3 -> x0, starting transfers between devices: 34.1 us -> none  [the longest x1 13 us: local(): lax.all_to_all(labels, 'grp', split_axis=0, concat_axis=0, tiled=True)]
    scatter x3 -> x0, local copies, waits for them, and re-layouts: 11.5 us -> none  [the longest x1 6.83 us: local(): jnp.zeros((cell_count, feat_dim), jnp.bfloat16).at[cell_index]]
  transfers between devices with their start and end apart: 8 -> 0, of which waited for: 7 -> 0; matrix products, arithmetic and copies ran while one was open for 2% -> 0% of each run, Pallas kernels for 0% -> 0%
where the time goes in v1:
time: 126 us; the launch traced here: 125 us
  Pallas kernels  122 us (97%)
  local copies, waits for them, and re-layouts  2.7 us (2%)
    pallas_call x1, Pallas kernels, local(): pl.pallas_call(kernel, out_shape=jax.ShapeDtypeStruct((1, ROWS), F32), in...  122 us
    unnamed x4, local copies, waits for them, and re-layouts  2.7 us

profile of v1, /device:TPU:2, one launch (start us, length us, event | category | flops | bytes accessed | tf_op | source)
XLA Modules:
  0.0 124.6 jit_solution(16121773265909398721)
XLA Ops:
  0.0 1.5 %copy.4.sca = f32[256,8]{1,0:T(8,128)} copy(f32[256,8]{0,1:T(8,128)} %param.5) | data formatting | bytes 16384 | tf_op args[1]
  1.5 121.9 %shard_map.37 = f32[1,256]{1,0:T(1,128)} custom-call(bf16[256,1024]{1,0:T(8,128)(2,1)} %emb.1, f32[256,8]{1,0:T(8,128)} %copy.4.sca, s32[1,256]{1,0:T(1,128)} %bitcast.3), custom_call_target="tpu_custom_call" | custom-call | tf_op jit(solution)/shard_map/pallas_call | solution.py:500
  123.4 0.0 copy-start
  123.4 0.7 copy-done
  124.1 0.6 copy.6
Async XLA Ops:
  123.4 0.7 copy-start
